TPU v7x, 512 devices: a whole 4x8x8 slice. The times are simulated.
512 devices in a mesh: dp: 16 (over z_hi, x), seq: 32 (over y, z_lo, core).
Axes of the slice: x: 4, y: 8, z: 8 (z_hi: 4, z_lo: 2; z = z_hi * 2 + z_lo), core: 2. Of those that a mesh axis runs over, the one named last changes fastest.
Arguments:
- frame_features: bfloat16 [32, 4, 64, 32, 512], P('dp', None, 'seq'), may hold values from -6 to 6
- conv_weight: bfloat16 [27, 512, 32], replicated, may hold values from -0.0546875 to 0.0546875
- conv_bias: float32 [32], replicated, may hold values from -0.5 to 0.5
- vae_noise: float32 [32, 2048, 64], P('dp', 'seq'), may hold values from -6 to 6
- flow_noise: float32 [32, 2048, 64], P('dp', 'seq'), may hold values from -6 to 6
- head_queries: bfloat16 [32, 2048, 2048], P('dp', 'seq'), may hold values from -48 to 48
- head_keys: bfloat16 [32, 2048, 2048], P('dp', 'seq'), may hold values from -48 to 48
- head_values: bfloat16 [32, 2048, 2048], P('dp', 'seq'), may hold values from -6 to 6
- out_weight: bfloat16 [2048, 64], replicated, may hold values from -0.125 to 0.125
- out_bias: float32 [64], replicated, may hold values from -1 to 1
Outputs:
- grad_queries: bfloat16 [32, 2048, 2048], P('dp', 'seq')
- grad_keys: bfloat16 [32, 2048, 2048], P('dp', 'seq')
- grad_values: bfloat16 [32, 2048, 2048], P('dp', 'seq')
- grad_out_weight: float32 [2048, 64], P('seq')
All inputs are finite; a program needn't handle non-finite values.
Results may differ from a plain program's by a relative error of at most 0.019.
Values may be sent and summed in bfloat16 or wider, within the bound.
No kernel may reach another device: no remote copies, remote signals or barrier semaphores. Data moves between devices by JAX's collectives and lax.ppermute only.
A program may use at most 64 MiB of HBM per device.

v0:
```python
import math

import jax
import jax.numpy as jnp
from jax import lax
from jax.sharding import PartitionSpec as P

HEADS = 16
HDIM = 128
LATC = 16


latent_factor = 0.476986


def extended(x, sides, width):
    for axis, dim in sides:
        peers, length = (lax.axis_size(axis), x.shape[dim])
        up = [(i, (i + 1) % peers) for i in range(peers - 1)]
        down = [(j, i) for i, j in up]
        last = lax.slice_in_dim(x, length - width, length, axis=dim)
        leading = lax.slice_in_dim(x, 0, width, axis=dim)
        before = lax.ppermute(last, axis, up)
        after = lax.ppermute(leading, axis, down)
        x = jnp.concatenate([before, x, after], axis=dim)
    return x


def causal_conv(padded_rows, conv_weight, conv_bias):
    clip_count, frame_count, padded_height, column_count, channels = padded_rows.shape
    row_count = padded_height - 2
    opening = padded_rows[:, :1]
    timed = jnp.concatenate([opening, opening, padded_rows], axis=1)
    border = jnp.zeros((clip_count, frame_count + 2, padded_height, 1, channels), padded_rows.dtype)
    framed = jnp.concatenate([border, timed, border], axis=3)
    out_channels = conv_weight.shape[2]
    summed = jnp.zeros(
        (clip_count * frame_count * row_count * column_count, out_channels), jnp.float32
    )
    for frame_tap in range(3):
        for row_tap in range(3):
            for column_tap in range(3):
                window = framed[
                    :,
                    frame_tap : frame_tap + frame_count,
                    row_tap : row_tap + row_count,
                    column_tap : column_tap + column_count,
                ]
                summed = summed + jnp.dot(
                    window.reshape(-1, channels),
                    conv_weight[frame_tap * 9 + row_tap * 3 + column_tap],
                    preferred_element_type=jnp.float32,
                )
    summed = summed + conv_bias
    return summed.reshape(clip_count, frame_count, row_count, column_count, out_channels)


def to_tokens(grid):
    clip_count, frame_count, row_count, column_count, channels = grid.shape
    shaped = grid.reshape(
        clip_count, frame_count, row_count // 2, 2, column_count // 2, 2, channels
    )
    shaped = shaped.transpose(0, 2, 1, 4, 6, 3, 5)
    return shaped.reshape(
        clip_count, row_count // 2 * frame_count * (column_count // 2), channels * 4
    )


def make_target(encoded, vae_noise, flow_noise):
    mean_tokens = to_tokens(encoded[..., :LATC])
    logvar_tokens = to_tokens(encoded[..., LATC:])
    latent = mean_tokens + jnp.exp(0.5 * logvar_tokens) * vae_noise
    return flow_noise - latent_factor * latent


def to_pairs(token_array, head_blocks):
    clip_count, row_count, total_width = token_array.shape
    block_width = total_width // head_blocks
    shaped = token_array.reshape(clip_count, row_count, head_blocks, block_width).transpose(
        2, 0, 1, 3
    )
    return shaped.reshape(head_blocks * clip_count, row_count, block_width)


def from_pairs(received, clip_count):
    source_count, row_count, block_width = received.shape
    head_blocks = source_count // clip_count
    shaped = received.reshape(head_blocks, clip_count, row_count, block_width).transpose(1, 2, 0, 3)
    return shaped.reshape(clip_count, row_count, head_blocks * block_width)


def shards(
    frame_features,
    conv_weight,
    conv_bias,
    vae_noise,
    flow_noise,
    head_queries,
    head_keys,
    head_values,
    out_weight,
    out_bias,
):
    rank_count = lax.axis_size("seq")
    clip_count, dev_tokens, full_width = head_queries.shape
    feature_count = out_weight.shape[1]
    score_scale = 1.0 / math.sqrt(HDIM)
    activated = jax.nn.silu(frame_features.astype(jnp.float32)).astype(jnp.bfloat16)
    padded = extended(activated, (("seq", 2),), 1)
    encoded = causal_conv(padded, conv_weight, conv_bias)
    target = make_target(encoded, vae_noise, flow_noise)
    head_blocks = rank_count // clip_count
    pair_heads = clip_count * HEADS // rank_count
    pair_width = pair_heads * HDIM
    clip_rows = rank_count * dev_tokens
    block_rows = min(512, clip_rows)
    block_count = clip_rows // block_rows

    def forward_clip(query_piece, key_pair, value_pair):
        scores = (
            jnp.einsum("qhd,khd->hqk", query_piece, key_pair, preferred_element_type=jnp.float32)
            * score_scale
        )
        shifted = jnp.exp(scores - jnp.max(scores, axis=-1, keepdims=True))
        attn_probs = (shifted / jnp.sum(shifted, axis=-1, keepdims=True)).astype(jnp.bfloat16)
        attended = jnp.einsum(
            "hqk,khd->qhd", attn_probs, value_pair, preferred_element_type=jnp.float32
        ).astype(jnp.bfloat16)
        return (attn_probs, attended)

    got_queries, got_keys, got_values = (
        lax.all_to_all(
            to_pairs(head_queries, head_blocks), "seq", split_axis=0, concat_axis=0, tiled=True
        ),
        lax.all_to_all(
            to_pairs(head_keys, head_blocks), "seq", split_axis=0, concat_axis=0, tiled=True
        ),
        lax.all_to_all(
            to_pairs(head_values, head_blocks), "seq", split_axis=0, concat_axis=0, tiled=True
        ),
    )
    query_pair = got_queries.reshape(block_count, block_rows, pair_heads, HDIM)
    key_pair = got_keys.reshape(clip_rows, pair_heads, HDIM)
    value_pair = got_values.reshape(clip_rows, pair_heads, HDIM)

    def forward_block(query_piece):
        return forward_clip(query_piece, key_pair, value_pair)

    attn_probs, attended = lax.map(forward_block, query_pair)
    attended_flat = attended.reshape(clip_rows, pair_width)
    attended_back = lax.all_to_all(
        attended_flat.reshape(rank_count, dev_tokens, pair_width),
        "seq",
        split_axis=0,
        concat_axis=0,
        tiled=True,
    )
    attended_tokens = from_pairs(attended_back, clip_count).reshape(-1, full_width)
    predicted = jnp.dot(attended_tokens, out_weight, preferred_element_type=jnp.float32) + out_bias
    errors = (predicted.reshape(clip_count, dev_tokens, feature_count) - target).astype(
        jnp.bfloat16
    )
    errors_flat = errors.reshape(-1, feature_count)
    grad_tokens = jnp.einsum(
        "tp,wp->tw", errors_flat, out_weight, preferred_element_type=jnp.float32
    ).astype(jnp.bfloat16)
    grad_tokens = grad_tokens.reshape(clip_count, dev_tokens, full_width)
    grad_got = lax.all_to_all(
        to_pairs(grad_tokens, head_blocks), "seq", split_axis=0, concat_axis=0, tiled=True
    )
    grad_attended = grad_got.reshape(clip_rows, pair_width)
    weight_rows = lax.psum_scatter(
        jnp.einsum(
            "tw,tp->wp", attended_tokens, errors_flat, preferred_element_type=jnp.float32
        ).astype(jnp.bfloat16),
        "seq",
        scatter_dimension=0,
        tiled=True,
    ).astype(jnp.float32)
    grad_pair = grad_attended.reshape(block_count, block_rows, pair_heads, HDIM)

    def backward_block(carry, block_items):
        key_total, value_total = carry
        query_piece, probs_piece, attended_piece, grad_piece = block_items
        grad_probs = jnp.einsum(
            "qhd,khd->hqk", grad_piece, value_pair, preferred_element_type=jnp.float32
        )
        row_dots = jnp.sum(
            grad_piece.astype(jnp.float32) * attended_piece.astype(jnp.float32), axis=-1
        )
        grad_scores = (
            probs_piece.astype(jnp.float32) * (grad_probs - row_dots.T[:, :, None])
        ).astype(jnp.bfloat16)
        grad_query = (
            jnp.einsum("hqk,khd->qhd", grad_scores, key_pair, preferred_element_type=jnp.float32)
            * score_scale
        ).astype(jnp.bfloat16)
        key_part = (
            jnp.einsum("hqk,qhd->khd", grad_scores, query_piece, preferred_element_type=jnp.float32)
            * score_scale
        )
        value_part = jnp.einsum(
            "hqk,qhd->khd", probs_piece, grad_piece, preferred_element_type=jnp.float32
        )
        return ((key_total + key_part, value_total + value_part), grad_query)

    zero_total = jnp.zeros((clip_rows, pair_heads, HDIM), jnp.float32)
    totals, grad_query = lax.scan(
        backward_block, (zero_total, zero_total), (query_pair, attn_probs, attended, grad_pair)
    )
    query_send = grad_query.reshape(rank_count, dev_tokens, pair_width)
    key_send = totals[0].astype(jnp.bfloat16).reshape(rank_count, dev_tokens, pair_width)
    value_send = totals[1].astype(jnp.bfloat16).reshape(rank_count, dev_tokens, pair_width)
    query_back, key_back, value_back = (
        lax.all_to_all(query_send, "seq", split_axis=0, concat_axis=0, tiled=True),
        lax.all_to_all(key_send, "seq", split_axis=0, concat_axis=0, tiled=True),
        lax.all_to_all(value_send, "seq", split_axis=0, concat_axis=0, tiled=True),
    )
    grad_queries = from_pairs(query_back, clip_count)
    grad_keys = from_pairs(key_back, clip_count)
    grad_values = from_pairs(value_back, clip_count)
    grad_out_weight = lax.psum(weight_rows, "dp")
    return (grad_queries, grad_keys, grad_values, grad_out_weight)


def solution(mesh):
    return jax.shard_map(
        shards,
        mesh=mesh,
        in_specs=(
            P("dp", None, "seq", None, None),
            P(),
            P(),
            P("dp", "seq", None),
            P("dp", "seq", None),
            P("dp", "seq", None),
            P("dp", "seq", None),
            P("dp", "seq", None),
            P(),
            P(),
        ),
        out_specs=(
            P("dp", "seq", None),
            P("dp", "seq", None),
            P("dp", "seq", None),
            P("seq", None),
        ),
        check_vma=False,
    )
```

profile of v0, /device:TPU:32, one launch (start us, length us, event | category | flops | bytes accessed | tf_op | source)
XLA Modules:
  0.0 491.9 jit_solution(6019694938056784839)
XLA Ops:
  7.2 1.4 fusion.57
  9.4 2.0 collective-permute-start
  11.4 5.8 %collective-permute-start.1 = (bf16[2,4,1,32,512]{4,3,2,1,0:T(8,128)(2,1)S(1)}, bf16[2,4,1,32,512]{4,3,2,1,0:T(8,128)(2,1)S(1)}, u32[]{:S(2)}, u32[]{:S(2)}) collective-permute-start(bf16[2,4,1,32,512]{4,3,2,1,0:T(8,128)(2,1)S(1)} %get-tuple-element.234), channel_id=1, source_target_pairs={{1,0},{2,1},{3,2},{4,3},{5,4},{6,5},{7,6},{8,7},{9,8},{10,9},{11,1... | collective-permute-start | bytes 786440 | tf_op jit(solution)/shard_map/ppermute | solution.py:24
  18.1 7.4 %all-to-all-start = ((bf16[32,64,128]{2,1,0:T(8,128)(2,1)}), bf16[32,64,128]{2,1,0:T(8,128)(2,1)S(1)}, u32[]{:S(2)}, u32[]{:S(2)}) async-start(bf16[32,64,128]{2,1,0:T(8,128)(2,1)} %bitcast.9), calls=%async_computation | async-start | bytes 1048576 | tf_op jit(solution)/shard_map/all_to_all | solution.py:132
  28.2 1.5 copy.47
  33.3 5.8 %pad_slice_fusion.1 = (bf16[2,4,2,32,512]{4,3,2,1,0:T(8,128)(2,1)}, bf16[2,4,2,32,512]{4,3,2,1,0:T(8,128)(2,1)S(1)}, bf16[2,4,2,32,512]{4,3,2,1,0:T(8,128)(2,1)S...) fusion(bf16[2,6,4,32,512]{4,3,2,1,0:T(8,128)(2,1)S(1)} %maximum, ...), kind=kLoop, calls=%fused_computation.41 | loop fusion | bytes 12582912 | tf_op jit(solution)/shard_map/slice | solution.py:43
  53.4 8.3 %all-to-all-start.1 = ((bf16[32,64,128]{2,1,0:T(8,128)(2,1)}), bf16[32,64,128]{2,1,0:T(8,128)(2,1)S(1)}, u32[]{:S(2)}, u32[]{:S(2)}) async-start(bf16[32,64,128]{2,1,0:T(8,128)(2,1)} %bitcast.361), calls=%async_computation.1 | async-start | bytes 1048576 | tf_op jit(solution)/shard_map/all_to_all | solution.py:135
  61.7 1.2 maximum_maximum_fusion.1
  63.1 1.6 fusion.83
  64.8 1.6 fusion.89
  66.4 1.6 fusion.95
  68.1 7.1 %all-to-all-done.1 = bf16[32,64,128]{2,1,0:T(8,128)(2,1)S(1)} async-done(((bf16[32,64,128]{2,1,0:T(8,128)(2,1)}), bf16[32,64,128]{2,1,0:T(8,128)(2,1)S(1)}, u32[]{:S(2)}, u32[]{:S(2)}) %all-to-all-start.1) | async-done | bytes 524320 | tf_op jit(solution)/shard_map/all_to_all | solution.py:135
  75.1 8.8 %all-to-all-start.2 = ((bf16[32,64,128]{2,1,0:T(8,128)(2,1)}), bf16[32,64,128]{2,1,0:T(8,128)(2,1)}, u32[]{:S(2)}, u32[]{:S(2)}) async-start(bf16[32,64,128]{2,1,0:T(8,128)(2,1)} %bitcast.360), calls=%async_computation.2 | async-start | bytes 1048576 | tf_op jit(solution)/shard_map/all_to_all | solution.py:138
  83.9 1.8 pad_maximum_fusion.1
  86.8 1.6 fusion.113
  88.4 1.6 fusion.77
  90.1 1.6 fusion.64
  91.7 5.8 %all-to-all-done.2 = bf16[32,64,128]{2,1,0:T(8,128)(2,1)} async-done(((bf16[32,64,128]{2,1,0:T(8,128)(2,1)}), bf16[32,64,128]{2,1,0:T(8,128)(2,1)}, u32[]{:S(2)}, u32[]{:S(2)}) %all-to-all-start.2) | async-done | bytes 524320 | tf_op jit(solution)/shard_map/all_to_all | solution.py:138
  98.3 28.8 %while.27 = (s32[]{:T(128)}, bf16[4,1,512,2048]{3,2,1,0:T(8,128)(2,1)}, bf16[4,512,1,128]{3,1,2,0:T(8,128)(2,1)}, bf16[4,512,1,128]{3,1,2,0:T(8,128)(2,1)}, bf16...) while((s32[]{:T(128)}, bf16[4,1,512,2048]{3,2,1,0:T(8,128)(2,1)}, ...), condition=%wide.region_3.4_spmd, body=%wide.region_0.3_spmd.sunk | while | flops 546372608 | bytes 20196940 | solution.py:149
  98.3 1.8 multiply_reduce_fusion.4
  100.9 2.2 bitcast_dynamic-update-slice_fusion.2
  103.2 2.4 fusion.200
  105.6 1.7 multiply_reduce_fusion.4
  108.1 2.2 bitcast_dynamic-update-slice_fusion.2
  110.3 2.4 fusion.200
  112.7 1.7 multiply_reduce_fusion.4
  115.2 2.3 bitcast_dynamic-update-slice_fusion.2
  117.5 2.4 fusion.200
  119.9 1.7 multiply_reduce_fusion.4
  122.4 2.3 bitcast_dynamic-update-slice_fusion.2
  124.7 2.4 fusion.200
  127.1 8.5 %all-to-all-start.3 = ((bf16[32,64,128]{2,1,0:T(8,128)(2,1)}), bf16[32,64,128]{2,1,0:T(8,128)(2,1)S(1)}, u32[]{:S(2)}, u32[]{:S(2)}) async-start(bf16[32,64,128]{2,1,0:T(8,128)(2,1)} %bitcast.19), calls=%async_computation.3 | async-start | bytes 1048576 | tf_op jit(solution)/shard_map/all_to_all | solution.py:151
  137.8 1.7 fusion.49
  141.7 7.5 %all-to-all-done.3 = bf16[32,64,128]{2,1,0:T(8,128)(2,1)S(1)} async-done(((bf16[32,64,128]{2,1,0:T(8,128)(2,1)}), bf16[32,64,128]{2,1,0:T(8,128)(2,1)S(1)}, u32[]{:S(2)}, u32[]{:S(2)}) %all-to-all-start.3) | async-done | bytes 524320 | tf_op jit(solution)/shard_map/all_to_all | solution.py:151
  152.3 8.4 %all-to-all-start.4 = ((bf16[32,64,128]{2,1,0:T(8,128)(2,1)}), bf16[32,64,128]{2,1,0:T(8,128)(2,1)S(1)}, u32[]{:S(2)}, u32[]{:S(2)}) async-start(bf16[32,64,128]{2,1,0:T(8,128)(2,1)} %bitcast.81), calls=%async_computation.4 | async-start | bytes 1048576 | tf_op jit(solution)/shard_map/all_to_all | solution.py:168
  160.7 13.5 %all-to-all-done.4 = bf16[32,64,128]{2,1,0:T(8,128)(2,1)S(1)} async-done(((bf16[32,64,128]{2,1,0:T(8,128)(2,1)}), bf16[32,64,128]{2,1,0:T(8,128)(2,1)S(1)}, u32[]{:S(2)}, u32[]{:S(2)}) %all-to-all-start.4) | async-done | bytes 524320 | tf_op jit(solution)/shard_map/all_to_all | solution.py:168
  175.0 44.6 %while.28 = (s32[]{:T(128)}, f32[2048,1,128]{0,2,1:T(8,128)}, f32[2048,1,128]{0,2,1:T(8,128)}, bf16[4,512,1,128]{3,1,2,0:T(8,128)(2,1)}, bf16[4,512,1,128]{3,1,2...) while((s32[]{:T(128)}, f32[2048,1,128]{0,2,1:T(8,128)}, ...), condition=%wide.region_6.7_spmd.clone, body=%wide.region_4.6_spmd.clone.sunk | while | flops 1079639552 | bytes 20716732 | solution.py:208
  175.0 1.2 multiply_reduce_fusion.5
  176.2 2.5 multiply_convert_fusion.2
  178.8 2.4 fusion.209
  181.1 1.4 fusion.211
  182.5 3.2 fusion.210
  185.7 1.2 multiply_reduce_fusion.5
  186.9 2.5 multiply_convert_fusion.2
  189.4 2.8 fusion.209
  192.2 1.4 fusion.211
  193.5 3.4 fusion.210
  197.0 1.2 multiply_reduce_fusion.5
  198.2 2.5 multiply_convert_fusion.2
  200.7 2.8 fusion.209
  203.5 1.4 fusion.211
  204.9 3.4 fusion.210
  208.3 1.2 multiply_reduce_fusion.5
  209.5 2.5 multiply_convert_fusion.2
  212.0 2.8 fusion.209
  214.8 1.4 fusion.211
  216.2 3.4 fusion.210
  219.6 2.3 copy.56
  221.9 8.4 %all-to-all-start.7 = ((bf16[32,64,128]{2,1,0:T(8,128)(2,1)}), bf16[32,64,128]{2,1,0:T(8,128)(2,1)S(1)}, u32[]{:S(2)}, u32[]{:S(2)}) async-start(bf16[32,64,128]{2,1,0:T(8,128)(2,1)} %bitcast.90), calls=%async_computation.7 | async-start | bytes 1048576 | tf_op jit(solution)/shard_map/all_to_all | solution.py:217
  230.6 13.2 %all-to-all-done.7 = bf16[32,64,128]{2,1,0:T(8,128)(2,1)S(1)} async-done(((bf16[32,64,128]{2,1,0:T(8,128)(2,1)}), bf16[32,64,128]{2,1,0:T(8,128)(2,1)S(1)}, u32[]{:S(2)}, u32[]{:S(2)}) %all-to-all-start.7) | async-done | bytes 524320 | tf_op jit(solution)/shard_map/all_to_all | solution.py:217
  243.8 20.9 %all_to_all.40 = bf16[32,64,128]{2,1,0:T(8,128)(2,1)S(1)} all-to-all(bf16[32,64,128]{2,1,0:T(8,128)(2,1)S(1)} %bitcast.357), channel_id=1, replica_groups=mesh['dp'=16,'seq'=32] {'seq'}, dimensions={0} | all-to-all | bytes 1048576 | tf_op jit(solution)/shard_map/all_to_all | solution.py:216
  264.7 8.4 %all-to-all-start.5 = ((bf16[32,64,128]{2,1,0:T(8,128)(2,1)}), bf16[32,64,128]{2,1,0:T(8,128)(2,1)S(1)}, u32[]{:S(2)}, u32[]{:S(2)}) async-start(bf16[32,64,128]{2,1,0:T(8,128)(2,1)} %bitcast.366), calls=%async_computation.5 | async-start | bytes 1048576 | tf_op jit(solution)/shard_map/all_to_all | solution.py:215
  274.3 124.8 %reduce-scatter.2.cloned.1.call-done = bf16[64,64]{1,0:T(8,128)(2,1)} async-done(((bf16[2048,64]{1,0:T(8,128)(2,1)}), bf16[64,64]{1,0:T(8,128)(2,1)}) %reduce-scatter.2.cloned.1.call-update) | async-done | bytes 8208 | tf_op jit(solution)/shard_map/reduce_scatter | solution.py:172
  399.1 83.1 %psum.7 = f32[64,64]{1,0:T(8,128)} all-reduce(bf16[64,64]{1,0:T(8,128)(2,1)} %reduce-scatter.2.cloned.1.call-done), channel_id=1, replica_groups=mesh['dp'=16,'seq'=32] {'dp'}, use_global_device_ids=true, to_apply=%region_8.9 | all-reduce | flops 4096 | bytes 24576 | tf_op jit(solution)/shard_map/psum | solution.py:222
  (130 shorter events, 40.0 us)
Async XLA Ops:
  7.2 10.0 %copy-start = (bf16[2,64,2048]{2,1,0:T(8,128)(2,1)S(1)}, bf16[2,64,2048]{2,1,0:T(8,128)(2,1)}, u32[]{:S(2)}) copy-start(bf16[2,64,2048]{2,1,0:T(8,128)(2,1)} %param.19) | copy-start | bytes 1572868
  7.2 18.3 %copy-start.14 = (bf16[2,64,2048]{2,1,0:T(8,128)(2,1)S(1)}, bf16[2,64,2048]{2,1,0:T(8,128)(2,1)}, u32[]{:S(2)}) copy-start(bf16[2,64,2048]{2,1,0:T(8,128)(2,1)} %param.20) | copy-start | bytes 1572868
  9.4 18.1 %copy-start.24 = (f32[2,64,64]{2,1,0:T(8,128)S(1)}, f32[2,64,64]{2,1,0:T(8,128)}, u32[]{:S(2)}) copy-start(f32[2,64,64]{2,1,0:T(8,128)} %param.17) | copy-start | bytes 98308
  9.4 20.4 %copy-start.15 = (bf16[2,64,2048]{2,1,0:T(8,128)(2,1)S(1)}, bf16[2,64,2048]{2,1,0:T(8,128)(2,1)}, u32[]{:S(2)}) copy-start(bf16[2,64,2048]{2,1,0:T(8,128)(2,1)} %param.21) | copy-start | bytes 1572868
  9.4 21.3 %collective-permute-start = (bf16[2,4,1,32,512]{4,3,2,1,0:T(8,128)(2,1)}, bf16[2,4,1,32,512]{4,3,2,1,0:T(8,128)(2,1)S(1)}, u32[]{:S(2)}, u32[]{:S(2)}) collective-permute-start(bf16[2,4,1,32,512]{4,3,2,1,0:T(8,128)(2,1)} %get-tuple-element.233), channel_id=1, source_target_pairs={{0,1},{1,2},{2,3},{3,4},{4,5},{5,6},{6,7},{7,8},{8,9},{9,10},{10,1... | collective-permute-start | bytes 786440 | tf_op jit(solution)/shard_map/ppermute | solution.py:23
  11.4 19.3 %collective-permute-start.1 = (bf16[2,4,1,32,512]{4,3,2,1,0:T(8,128)(2,1)S(1)}, bf16[2,4,1,32,512]{4,3,2,1,0:T(8,128)(2,1)S(1)}, u32[]{:S(2)}, u32[]{:S(2)}) collective-permute-start(bf16[2,4,1,32,512]{4,3,2,1,0:T(8,128)(2,1)S(1)} %get-tuple-element.234), channel_id=1, source_target_pairs={{1,0},{2,1},{3,2},{4,3},{5,4},{6,5},{7,6},{8,7},{9,8},{10,9},{11,1... | collective-permute-start | bytes 786440 | tf_op jit(solution)/shard_map/ppermute | solution.py:24
  18.1 34.5 %all-to-all-start = ((bf16[32,64,128]{2,1,0:T(8,128)(2,1)}), bf16[32,64,128]{2,1,0:T(8,128)(2,1)S(1)}, u32[]{:S(2)}, u32[]{:S(2)}) async-start(bf16[32,64,128]{2,1,0:T(8,128)(2,1)} %bitcast.9), calls=%async_computation | async-start | bytes 1048576 | tf_op jit(solution)/shard_map/all_to_all | solution.py:132
  30.7 0.7 copy-start.5
  31.5 0.7 copy-start.6
  33.3 5.8 %copy-start.13 = (bf16[27,512,32]{1,2,0:T(8,128)(2,1)S(1)}, bf16[27,512,32]{1,2,0:T(8,128)(2,1)}, u32[]{:S(2)}) copy-start(bf16[27,512,32]{1,2,0:T(8,128)(2,1)} %param.15) | copy-start | bytes 2654212
  52.6 0.8 copy-start.4
  53.4 21.7 %all-to-all-start.1 = ((bf16[32,64,128]{2,1,0:T(8,128)(2,1)}), bf16[32,64,128]{2,1,0:T(8,128)(2,1)S(1)}, u32[]{:S(2)}, u32[]{:S(2)}) async-start(bf16[32,64,128]{2,1,0:T(8,128)(2,1)} %bitcast.361), calls=%async_computation.1 | async-start | bytes 1048576 | tf_op jit(solution)/shard_map/all_to_all | solution.py:135
  75.1 22.3 %all-to-all-start.2 = ((bf16[32,64,128]{2,1,0:T(8,128)(2,1)}), bf16[32,64,128]{2,1,0:T(8,128)(2,1)}, u32[]{:S(2)}, u32[]{:S(2)}) async-start(bf16[32,64,128]{2,1,0:T(8,128)(2,1)} %bitcast.360), calls=%async_computation.2 | async-start | bytes 1048576 | tf_op jit(solution)/shard_map/all_to_all | solution.py:138
  85.7 4.3 copy-start.9
  98.3 37.3 %copy-start.8 = (bf16[2,4,2,32,512]{4,3,2,1,0:T(8,128)(2,1)S(1)}, bf16[2,4,2,32,512]{4,3,2,1,0:T(8,128)(2,1)}, u32[]{:S(2)}) copy-start(bf16[2,4,2,32,512]{4,3,2,1,0:T(8,128)(2,1)} %get-tuple-element.215) | copy-start | bytes 1572868
  98.3 38.4 %copy-start.12 = (bf16[2,4,2,32,512]{4,3,2,1,0:T(8,128)(2,1)S(1)}, bf16[2,4,2,32,512]{4,3,2,1,0:T(8,128)(2,1)}, u32[]{:S(2)}) copy-start(bf16[2,4,2,32,512]{4,3,2,1,0:T(8,128)(2,1)} %get-tuple-element.232) | copy-start | bytes 1572868
  127.1 10.6 %copy-start.17 = (f32[512,32]{0,1:T(8,128)S(1)}, f32[512,32]{0,1:T(8,128)}, u32[]{:S(2)}) copy-start(f32[512,32]{0,1:T(8,128)} %fusion.103) | copy-start | bytes 196612
  127.1 10.7 %copy-start.18 = (f32[512,32]{0,1:T(8,128)S(1)}, f32[512,32]{0,1:T(8,128)}, u32[]{:S(2)}) copy-start(f32[512,32]{0,1:T(8,128)} %fusion.105) | copy-start | bytes 196612
  127.1 10.7 %copy-start.19 = (f32[512,32]{0,1:T(8,128)S(1)}, f32[512,32]{0,1:T(8,128)}, u32[]{:S(2)}) copy-start(f32[512,32]{0,1:T(8,128)} %fusion.107) | copy-start | bytes 196612
  127.1 10.7 %copy-start.20 = (f32[512,32]{0,1:T(8,128)S(1)}, f32[512,32]{0,1:T(8,128)}, u32[]{:S(2)}) copy-start(f32[512,32]{0,1:T(8,128)} %fusion.109) | copy-start | bytes 196612
  127.1 12.4 %copy-start.7 = (bf16[2,4,2,32,512]{4,3,2,1,0:T(8,128)(2,1)S(1)}, bf16[2,4,2,32,512]{4,3,2,1,0:T(8,128)(2,1)}, u32[]{:S(2)}) copy-start(bf16[2,4,2,32,512]{4,3,2,1,0:T(8,128)(2,1)} %get-tuple-element.207) | copy-start | bytes 1572868
  127.1 12.4 %copy-start.25 = (f32[32]{0:T(128)S(1)}, f32[32]{0:T(128)}, u32[]{:S(2)}) copy-start(f32[32]{0:T(128)} %param.16) | copy-start | bytes 388
  127.1 22.0 %all-to-all-start.3 = ((bf16[32,64,128]{2,1,0:T(8,128)(2,1)}), bf16[32,64,128]{2,1,0:T(8,128)(2,1)S(1)}, u32[]{:S(2)}, u32[]{:S(2)}) async-start(bf16[32,64,128]{2,1,0:T(8,128)(2,1)} %bitcast.19), calls=%async_computation.3 | async-start | bytes 1048576 | tf_op jit(solution)/shard_map/all_to_all | solution.py:151
  135.7 3.9 copy-start.21
  140.6 9.7 %copy-start.16 = (bf16[2048,64]{0,1:T(8,128)(2,1)S(1)}, bf16[2048,64]{0,1:T(8,128)(2,1)}, u32[]{:S(2)}) copy-start(bf16[2048,64]{0,1:T(8,128)(2,1)} %param.22) | copy-start | bytes 786436
  140.6 9.7 %copy-start.26 = (f32[64]{0:T(128)S(1)}, f32[64]{0:T(128)}, u32[]{:S(2)}) copy-start(f32[64]{0:T(128)} %param.23) | copy-start | bytes 772
  140.9 9.8 %copy-start.22 = (f32[2,64,64]{1,2,0:T(8,128)S(1)}, f32[2,64,64]{1,2,0:T(8,128)}, u32[]{:S(2)}) copy-start(f32[2,64,64]{1,2,0:T(8,128)} %copy.46) | copy-start | bytes 98308
  140.9 9.8 %copy-start.23 = (f32[2,64,64]{1,2,0:T(8,128)S(1)}, f32[2,64,64]{1,2,0:T(8,128)}, u32[]{:S(2)}) copy-start(f32[2,64,64]{1,2,0:T(8,128)} %copy.47) | copy-start | bytes 98308
  149.5 0.8 copy-start.10
  152.3 21.9 %all-to-all-start.4 = ((bf16[32,64,128]{2,1,0:T(8,128)(2,1)}), bf16[32,64,128]{2,1,0:T(8,128)(2,1)S(1)}, u32[]{:S(2)}, u32[]{:S(2)}) async-start(bf16[32,64,128]{2,1,0:T(8,128)(2,1)} %bitcast.81), calls=%async_computation.4 | async-start | bytes 1048576 | tf_op jit(solution)/shard_map/all_to_all | solution.py:168
  175.0 1.2 copy-start.2
  182.5 3.2 copy-start.3
  185.7 1.2 copy-start.2
  193.5 3.4 copy-start.3
  197.0 1.2 copy-start.2
  204.9 3.4 copy-start.3
  208.3 1.2 copy-start.2
  216.2 3.4 copy-start.3
  219.6 10.7 %copy-start.1 = (f32[2048,1,128]{0,2,1:T(8,128)S(1)}, f32[2048,1,128]{0,2,1:T(8,128)}, u32[]{:S(2)}) copy-start(f32[2048,1,128]{0,2,1:T(8,128)} %get-tuple-element.94) | copy-start | bytes 3145732
  221.9 21.9 %all-to-all-start.7 = ((bf16[32,64,128]{2,1,0:T(8,128)(2,1)}), bf16[32,64,128]{2,1,0:T(8,128)(2,1)S(1)}, u32[]{:S(2)}, u32[]{:S(2)}) async-start(bf16[32,64,128]{2,1,0:T(8,128)(2,1)} %bitcast.90), calls=%async_computation.7 | async-start | bytes 1048576 | tf_op jit(solution)/shard_map/all_to_all | solution.py:217
  230.3 42.9 %copy-start.11 = (bf16[2,64,16,128]{3,2,1,0:T(8,128)(2,1)S(1)}, bf16[2,64,16,128]{3,2,1,0:T(8,128)(2,1)}, u32[]{:S(2)}) copy-start(bf16[2,64,16,128]{3,2,1,0:T(8,128)(2,1)} %copy-done.10) | copy-start | bytes 1572868
  264.7 219.4 %all-to-all-start.5 = ((bf16[32,64,128]{2,1,0:T(8,128)(2,1)}), bf16[32,64,128]{2,1,0:T(8,128)(2,1)S(1)}, u32[]{:S(2)}, u32[]{:S(2)}) async-start(bf16[32,64,128]{2,1,0:T(8,128)(2,1)} %bitcast.366), calls=%async_computation.5 | async-start | bytes 1048576 | tf_op jit(solution)/shard_map/all_to_all | solution.py:215
  273.1 126.0 %reduce-scatter.2.cloned.1.call-start = ((), (), s32[]{:S(2)}) async-start(), calls=%async_computation.9 | async-start | bytes 540672 | tf_op jit(solution)/shard_map/reduce_scatter | solution.py:172
Sparse Core Ops, SparseCore 0:
  277.3 121.8 reduce-scatter.1
where the time goes:
time: 494 us; the launch traced here: 492 us
  waiting for transfers between devices  172 us (35%)
  blocking collectives  104 us (21%)
  matrix products  87.2 us (18%)
  starting transfers between devices  65.9 us (13%)
  local copies, waits for them, and re-layouts  25.5 us (5%)
  other arithmetic  22.8 us (5%)
  between operations  14.5 us (3%)
    reduce_scatter x1, waiting for transfers between devices, shards(): lax.psum_scatter(jnp.einsum('tw,tp->wp', attended_tokens, errors_flat, pr...  125 us
    psum x1, blocking collectives, shards(): grad_out_weight = lax.psum(weight_rows, 'dp')  83.1 us
    dot_general x27, matrix products, causal_conv(): jnp.dot(window.reshape(-1, channels), conv_weight[frame_tap * 9 + row_tap...  29.2 us
    all_to_all x1, blocking collectives, shards(): lax.all_to_all(key_send, 'seq', split_axis=0, concat_axis=0, tiled=True)  20.9 us
    dot_general x4, matrix products, backward_block(): jnp.einsum('hqk,qhd->khd', probs_piece, grad_piece, preferred_element_typ...  13.5 us
    all_to_all x1, waiting for transfers between devices, shards(): lax.all_to_all(to_pairs(grad_tokens, head_blocks), 'seq', split_axis=0, c...  13.5 us
    all_to_all x1, waiting for transfers between devices, shards(): lax.all_to_all(value_send, 'seq', split_axis=0, concat_axis=0, tiled=True)  13.2 us
    dot_general x4, matrix products, backward_block(): jnp.einsum('hqk,qhd->khd', grad_scores, query_piece, preferred_element_ty...  10.7 us
  transfers between devices with their start and end apart: 10, of which 6 were waited for; matrix products, arithmetic and copies ran while one was open for 10% of the time, Pallas kernels for 0%

commit v1 on v0

v1 whole, which is shorter than its diff:
```python
import math

import jax
import jax.numpy as jnp
from jax import lax
from jax.experimental import pallas as pl
from jax.experimental.pallas import tpu as pltpu
from jax.sharding import PartitionSpec as P

HEADS = 16
HDIM = 128
LATC = 16
RANKS = 32
TOK = 64
HALF = TOK // 2
SEQ = RANKS * TOK
FEAT = 64
SCALE = 1.0 / math.sqrt(HDIM)
EXP2_SCALE = SCALE * math.log2(math.e)
ROWS = 256
PIECES = ROWS // TOK
STEPS = SEQ // ROWS
BACK_ROWS = 512
SUB_BACK = 256
BACK_PIECES = BACK_ROWS // TOK
BACK_STEPS = SEQ // BACK_ROWS
latent_factor = 0.476986

NT = (((1,), (1,)), ((), ()))
TN = (((0,), (0,)), ((), ()))
F32 = jnp.float32
BF16 = jnp.bfloat16


def mm(a, b, dims=(((1,), (0,)), ((), ()))):
    return lax.dot_general(a, b, dims, preferred_element_type=F32)


def pack_kernel(q_ref, k_ref, v_ref, out_ref):
    for part, ref in enumerate((q_ref, k_ref, v_ref)):
        for head in range(HEADS):
            out_ref[head, 0, part] = ref[0, :, head * HDIM : (head + 1) * HDIM]


def pack(q, k, v):
    spec = pl.BlockSpec((1, TOK, HEADS * HDIM), lambda c: (c, 0, 0))
    return pl.pallas_call(
        pack_kernel,
        grid=(2,),
        in_specs=[spec] * 3,
        out_specs=pl.BlockSpec((HEADS, 1, 3, TOK, HDIM), lambda c: (0, c, 0, 0, 0)),
        out_shape=jax.ShapeDtypeStruct((HEADS, 2, 3, TOK, HDIM), BF16),
        name="pack",
    )(q, k, v).reshape(RANKS, 3, TOK, HDIM)


def unpack_kernel(in_ref, q_ref, k_ref, v_ref, sems):
    for part, ref in enumerate((q_ref, k_ref, v_ref)):
        for clip in range(2):
            for head in range(HEADS):
                pltpu.make_async_copy(
                    in_ref.at[head, clip, part],
                    ref.at[clip, :, pl.ds(head * HDIM, HDIM)],
                    sems.at[part],
                ).start()
    for part, ref in enumerate((q_ref, k_ref, v_ref)):
        pltpu.make_async_copy(ref, ref, sems.at[part]).wait()


def unpack(back):
    shape = jax.ShapeDtypeStruct((2, TOK, HEADS * HDIM), BF16)
    return pl.pallas_call(
        unpack_kernel,
        in_specs=[pl.BlockSpec(memory_space=pltpu.VMEM)],
        out_specs=[pl.BlockSpec(memory_space=pltpu.HBM)] * 3,
        out_shape=[shape] * 3,
        scratch_shapes=[pltpu.SemaphoreType.DMA((3,))],
        compiler_params=pltpu.CompilerParams(vmem_limit_bytes=16 << 20),
        name="unpack",
    )(back.reshape(HEADS, 2, 3, TOK, HDIM))


def conv_kernel(x_ref, w_ref, own_ref, next_ref, prev_ref):
    x = x_ref[...].astype(F32)
    act = (x / (1.0 + jnp.exp(-x))).astype(BF16)
    lane = lax.broadcasted_iota(jnp.int32, (32, 512), 1)
    col = lane & 31
    row = (lane >> 5) & 1
    frame = (lane >> 6) & 3
    summed = []
    for dy in range(3):
        timed = []
        for dt in range(3):
            taps = mm(w_ref[pl.ds((9 * dt + 3 * dy) * 32, 96), :], act, NT)
            left = jnp.where(col == 0, 0.0, pltpu.roll(taps[0:32], 1, 1))
            right = jnp.where(col == 31, 0.0, pltpu.roll(taps[64:96], 511, 1))
            timed.append(taps[32:64] + left + right)
        z0, z1, z2 = timed
        one = jnp.where(frame == 0, z1, pltpu.roll(z1, 64, 1))
        two = jnp.where(
            frame == 0, z0, jnp.where(frame == 1, pltpu.roll(z0, 64, 1), pltpu.roll(z0, 128, 1))
        )
        summed.append(z2 + one + two)
    down, here, up = summed
    down_own = pltpu.roll(down, 32, 1)
    up_own = pltpu.roll(up, 480, 1)
    own_ref[...] = here + jnp.where(row == 1, down_own, up_own)
    next_ref[...] = jnp.where(row == 0, pltpu.roll(down, 480, 1), 0.0)
    prev_ref[...] = jnp.where(row == 1, pltpu.roll(up, 32, 1), 0.0)


def conv(features, weight):
    shape = jax.ShapeDtypeStruct((32, 512), F32)
    return pl.pallas_call(
        conv_kernel,
        out_shape=[shape] * 3,
        compiler_params=pltpu.CompilerParams(vmem_limit_bytes=32 << 20),
        cost_estimate=pl.CostEstimate(
            flops=2 * 512 * 512 * 864, bytes_accessed=2 << 20, transcendentals=1 << 18
        ),
        name="conv",
    )(features, weight)


def forward_kernel(
    got_ref, w_ref, p_out, a_out, r_out, pred_out, p_buf, a_buf, r_buf, pred_buf, sems
):
    k = got_ref[:, 1].reshape(SEQ, HDIM)
    v = got_ref[:, 2].reshape(SEQ, HDIM)
    copies = []

    def send(i, kind, buf, out, per):
        part = pl.ds(i * per, per)
        copies.append(pltpu.make_async_copy(buf.at[part], out.at[part], sems.at[kind, i]))
        copies[-1].start()

    def scored(i):
        return mm(got_ref[pl.ds(i * PIECES, PIECES), 0].reshape(ROWS, HDIM), k, NT)

    def softmaxed(i, scores):
        top = jnp.max(scores, axis=-1, keepdims=True)
        probs = jnp.exp2((scores - top) * EXP2_SCALE)
        inverse = 1.0 / jnp.sum(probs, axis=-1, keepdims=True)
        p_buf[pl.ds(i * ROWS, ROWS)] = probs.astype(BF16)
        return inverse

    def finished(i, inverse):
        rows = pl.ds(i * ROWS, ROWS)
        attended = (mm(p_buf[rows], v) * inverse).astype(BF16)
        r_buf[rows] = jnp.broadcast_to(inverse, (ROWS, HDIM))
        a_buf[rows] = attended
        pieces = attended.reshape(PIECES, 2, HALF, HDIM)
        pred = mm(pieces[:, 0].reshape(PIECES * HALF, HDIM), w_ref[0])
        pred = pred + mm(pieces[:, 1].reshape(PIECES * HALF, HDIM), w_ref[1])
        pred_buf[pl.ds(i * PIECES, PIECES)] = pred.astype(BF16).reshape(PIECES, HALF, 2 * FEAT)
        send(i, 0, p_buf, p_out, ROWS)

    def sent(i):
        send(i, 1, pred_buf, pred_out, PIECES)
        send(i, 2, a_buf, a_out, ROWS)
        send(i, 3, r_buf, r_out, ROWS)

    scores, inverses = {0: scored(0)}, {}
    for i in range(STEPS + 2):
        if i + 1 < STEPS:
            scores[i + 1] = scored(i + 1)
        if i < STEPS:
            inverses[i] = softmaxed(i, scores.pop(i))
        if 1 <= i <= STEPS:
            finished(i - 1, inverses.pop(i - 1))
        if i >= 2:
            sent(i - 2)
    for copy in copies:
        copy.wait()


RESIDENT = pl.BlockSpec(memory_space=pltpu.VMEM)
STAYS = pl.BlockSpec(memory_space=pltpu.HBM)


def forward(got, weights):
    *kept, pred = pl.pallas_call(
        forward_kernel,
        in_specs=[RESIDENT, RESIDENT],
        out_specs=[STAYS] * 4,
        out_shape=[
            pltpu.HBM((SEQ, SEQ), BF16),
            pltpu.HBM((SEQ, HDIM), BF16),
            pltpu.HBM((SEQ, HDIM), F32),
            jax.ShapeDtypeStruct((RANKS, HALF, 2 * FEAT), BF16),
        ],
        scratch_shapes=[
            pltpu.VMEM((SEQ, SEQ), BF16),
            pltpu.VMEM((SEQ, HDIM), BF16),
            pltpu.VMEM((SEQ, HDIM), F32),
            pltpu.VMEM((RANKS, HALF, 2 * FEAT), BF16),
            pltpu.SemaphoreType.DMA((4, STEPS)),
        ],
        compiler_params=pltpu.CompilerParams(vmem_limit_bytes=40 << 20),
        cost_estimate=pl.CostEstimate(
            flops=4 * SEQ * SEQ * HDIM, bytes_accessed=12 << 20, transcendentals=SEQ * SEQ
        ),
        name="forward",
    )(got, weights)
    return [pltpu.with_memory_space_constraint(x, pltpu.HBM) for x in kept], pred


def errors_kernel(part_ref, first_ref, second_ref, out_ref):
    total = jnp.concatenate([first_ref[...], second_ref[...]], axis=0)
    for head in range(HEADS):
        total = total + part_ref[head].astype(F32)
    errors = total.astype(BF16)
    for head in range(HEADS):
        out_ref[head] = errors


def make_errors(parts, first, second):
    return pl.pallas_call(
        errors_kernel,
        out_shape=jax.ShapeDtypeStruct((HEADS, TOK, 2 * FEAT), BF16),
        compiler_params=pltpu.CompilerParams(vmem_limit_bytes=8 << 20),
        name="errors",
    )(parts, first, second)


def back_spec(width):
    return pl.BlockSpec((BACK_ROWS, width), lambda i: (i, 0))


def back_packed():
    return pl.BlockSpec((BACK_PIECES, HALF, 2 * FEAT), lambda i: (i, 0, 0))


def backward_kernel(got_ref, w_ref, p_ref, a_ref, r_ref, e_ref, out_ref, gw_ref, dk_acc, dv_acc, gs):
    step = pl.program_id(0)

    @pl.when(step == 0)
    def _():
        dk_acc[...] = jnp.zeros_like(dk_acc)
        dv_acc[...] = jnp.zeros_like(dv_acc)
        gw_ref[...] = jnp.zeros_like(gw_ref)

    q = got_ref[pl.ds(step * BACK_PIECES, BACK_PIECES), 0].reshape(BACK_ROWS, HDIM)
    k = got_ref[:, 1].reshape(SEQ, HDIM)
    v = got_ref[:, 2].reshape(SEQ, HDIM)
    errors = e_ref[...].reshape(BACK_PIECES * HALF, 2 * FEAT)
    first = mm(errors, w_ref[0], NT).reshape(BACK_PIECES, 1, HALF, HDIM)
    second = mm(errors, w_ref[1], NT).reshape(BACK_PIECES, 1, HALF, HDIM)
    grad = jnp.concatenate([first, second], axis=1).reshape(BACK_ROWS, HDIM) * r_ref[...]
    grad = grad.astype(BF16)
    attended = a_ref[...]
    dots = jnp.sum(grad.astype(F32) * attended.astype(F32), axis=-1, keepdims=True)

    def part(i):
        return slice(i * SUB_BACK, (i + 1) * SUB_BACK)

    def scored(i):
        return mm(grad[part(i)], v, NT)

    def weighted(i, grad_probs):
        out = (p_ref[part(i)].astype(F32) * (grad_probs - dots[part(i)])).astype(BF16)
        gs[part(i)] = out
        return out

    def finished(i, grad_scores):
        count = SUB_BACK // TOK
        dq = (mm(grad_scores, k) * SCALE).astype(BF16)
        out_ref[pl.ds(step * BACK_PIECES + i * count, count), 0] = dq.reshape(count, TOK, HDIM)

    subs = BACK_ROWS // SUB_BACK
    grad_probs, grad_scores = {0: scored(0)}, {}
    for i in range(subs + 1):
        if i + 1 < subs:
            grad_probs[i + 1] = scored(i + 1)
        if i < subs:
            grad_scores[i] = weighted(i, grad_probs.pop(i))
        if i >= 1:
            finished(i - 1, grad_scores.pop(i - 1))

    dv_acc[...] += mm(grad, p_ref[...], TN)
    dk_acc[...] += mm(q, gs[...], TN)
    pieces = attended.reshape(BACK_PIECES, 2, HALF, HDIM)
    lane = lax.broadcasted_iota(jnp.int32, (HDIM, 2 * FEAT), 1)
    low = mm(pieces[:, 0].reshape(BACK_PIECES * HALF, HDIM), errors, TN)
    high = mm(pieces[:, 1].reshape(BACK_PIECES * HALF, HDIM), errors, TN)
    gw_ref[...] += jnp.where(lane < FEAT, low, high)

    @pl.when(step == pl.num_programs(0) - 1)
    def _():
        out_ref[:, 1] = (dk_acc[...] * SCALE).astype(BF16).T.reshape(RANKS, TOK, HDIM)
        out_ref[:, 2] = dv_acc[...].astype(BF16).T.reshape(RANKS, TOK, HDIM)


def backward(got, weights, probs, attended, inverse, errors):
    return pl.pallas_call(
        backward_kernel,
        grid=(BACK_STEPS,),
        in_specs=[RESIDENT, RESIDENT, back_spec(SEQ), back_spec(HDIM), back_spec(HDIM), back_packed()],
        out_specs=[
            pl.BlockSpec((RANKS, 3, TOK, HDIM), lambda i: (0, 0, 0, 0)),
            pl.BlockSpec((HDIM, 2 * FEAT), lambda i: (0, 0)),
        ],
        out_shape=[
            jax.ShapeDtypeStruct((RANKS, 3, TOK, HDIM), BF16),
            jax.ShapeDtypeStruct((HDIM, 2 * FEAT), F32),
        ],
        scratch_shapes=[
            pltpu.VMEM((HDIM, SEQ), F32),
            pltpu.VMEM((HDIM, SEQ), F32),
            pltpu.VMEM((BACK_ROWS, SEQ), BF16),
        ],
        compiler_params=pltpu.CompilerParams(vmem_limit_bytes=40 << 20),
        cost_estimate=pl.CostEstimate(
            flops=8 * SEQ * SEQ * HDIM, bytes_accessed=14 << 20, transcendentals=0
        ),
        name="backward",
    )(got, weights, probs, attended, inverse, errors)


CLIP_RANKS = [list(range(clip, RANKS, 2)) for clip in range(2)]
PARTNER = [(i, i ^ 1) for i in range(RANKS)]


def exchange(x, groups=None):
    return lax.all_to_all(
        x, "seq", split_axis=0, concat_axis=0, axis_index_groups=groups, tiled=True
    )


def permute(x, pairs, axis="seq"):
    return lax.ppermute(x, axis, pairs)


def shards(
    frame_features,
    conv_weight,
    conv_bias,
    vae_noise,
    flow_noise,
    head_queries,
    head_keys,
    head_values,
    out_weight,
    out_bias,
):
    rank = lax.axis_index("seq")
    got = exchange(pack(head_queries, head_keys, head_values))

    own, to_next, to_prev = conv(
        frame_features.reshape(512, 512), conv_weight.transpose(0, 2, 1).reshape(864, 512)
    )
    up = [(i, i + 1) for i in range(RANKS - 1)]
    down = [(i + 1, i) for i in range(RANKS - 1)]
    halo = [lax.ppermute(to_next, "seq", up), lax.ppermute(to_prev, "seq", down)]

    head, clip = rank // 2, rank % 2
    head_weight = lax.dynamic_slice(out_weight, (head * HDIM, 0), (HDIM, FEAT))
    empty = jnp.zeros_like(head_weight)
    weights = jnp.stack(
        [
            jnp.concatenate([head_weight, empty], axis=1),
            jnp.concatenate([empty, head_weight], axis=1),
        ]
    )
    (probs, attended, inverse), pred = forward(got, weights)
    attended, own, halo = lax.optimization_barrier((attended, own, halo))
    encoded = own + halo[0] + halo[1]
    encoded = encoded + conv_bias[:, None]
    encoded = encoded.reshape(2, LATC, 2, 4, 2, 16, 2).transpose(0, 2, 3, 5, 1, 4, 6)
    mean_tokens, logvar_tokens = encoded.reshape(2, 2, TOK, FEAT)
    latent = mean_tokens + jnp.exp(0.5 * logvar_tokens) * vae_noise
    base = out_bias - (flow_noise - latent_factor * latent)
    base = base.reshape(2, 2, HALF, FEAT).transpose(0, 2, 1, 3).reshape(2, HALF, 2 * FEAT)
    mine = lax.dynamic_index_in_dim(base, clip, 0, False)
    theirs = permute(lax.dynamic_index_in_dim(base, 1 - clip, 0, False), PARTNER)
    first = jnp.where(clip == 0, mine, theirs)
    second = jnp.where(clip == 0, theirs, mine)

    parts = exchange(pred.reshape(HEADS, TOK, 2 * FEAT), CLIP_RANKS)
    errors = exchange(make_errors(parts, first, second), CLIP_RANKS)
    errors = errors.reshape(RANKS, HALF, 2 * FEAT)
    grads, weight_grad = backward(got, weights, probs, attended, inverse, errors)
    grad_queries, grad_keys, grad_values = unpack(exchange(grads))

    weight_grad = (weight_grad[:, :FEAT] + weight_grad[:, FEAT:]).reshape(2, FEAT, FEAT)
    mine = lax.dynamic_index_in_dim(weight_grad, clip, 0, False)
    theirs = lax.dynamic_index_in_dim(weight_grad, 1 - clip, 0, False)
    total = mine + permute(theirs, PARTNER)
    for bit in (1, 2, 4, 8):
        total = total + permute(total, [(i, i ^ bit) for i in range(16)], "dp")
    return (grad_queries, grad_keys, grad_values, total)


def solution(mesh):
    return jax.shard_map(
        shards,
        mesh=mesh,
        in_specs=(
            P("dp", None, "seq", None, None),
            P(),
            P(),
            P("dp", "seq", None),
            P("dp", "seq", None),
            P("dp", "seq", None),
            P("dp", "seq", None),
            P("dp", "seq", None),
            P(),
            P(),
        ),
        out_specs=(
            P("dp", "seq", None),
            P("dp", "seq", None),
            P("dp", "seq", None),
            P("seq", None),
        ),
        check_vma=False,
    )
```

time: 494 us -> 149 us (0.30)
  the two profiles are of different devices: /device:TPU:32 before, /device:TPU:4 now
where the time goes in v1:
time: 149 us
  waiting for transfers between devices  58.7 us (39%)
  starting transfers between devices  45.4 us (30%)
  Pallas kernels  25 us (17%)
  blocking collectives  14.5 us (10%)
  local copies, waits for them, and re-layouts  2.92 us (2%)
    all_to_all x3, waiting for transfers between devices, exchange(): lax.all_to_all(x, 'seq', split_axis=0, concat_axis=0, axis_index_groups=g...  44.9 us
    ppermute x6, starting transfers between devices, permute(): return lax.ppermute(x, axis, pairs)  24.6 us
    all_to_all x3, starting transfers between devices, exchange(): lax.all_to_all(x, 'seq', split_axis=0, concat_axis=0, axis_index_groups=g...  17.3 us
    all_to_all x1, blocking collectives, exchange(): lax.all_to_all(x, 'seq', split_axis=0, concat_axis=0, axis_index_groups=g...  14.5 us
    ppermute x6, waiting for transfers between devices, permute(): return lax.ppermute(x, axis, pairs)  13.7 us
    pallas_call x1, Pallas kernels, backward(): pl.pallas_call(backward_kernel, grid=(BACK_STEPS,), in_specs=[RESIDENT, R...  11.3 us
    pallas_call x1, Pallas kernels, forward(): pl.pallas_call(forward_kernel, in_specs=[RESIDENT, RESIDENT], out_specs=[...  8.18 us
  transfers between devices with their start and end apart: 11, of which 9 were waited for; matrix products, arithmetic and copies ran while one was open for 2% of the time, Pallas kernels for 7%

profile of v1, /device:TPU:4, one launch (start us, length us, event | category | flops | bytes accessed | tf_op | source)
XLA Modules:
  0.0 148.7 jit_solution(6063078297200134422)
XLA Ops:
  0.6 0.0 copy-start
  0.6 2.5 %pack.1 = bf16[16,2,3,64,128]{4,3,2,1,0:T(8,128)(2,1)} custom-call(bf16[2,64,2048]{2,1,0:T(8,128)(2,1)} %q_ref.1, bf16[2,64,2048]{2,1,0:T(8,128)(2,1)} %k_ref.1, bf16[2,64,2048]{2,1,0:T(8,128)(2,1)} %v_ref.1), custom_call_target="tpu_custom_call" | custom-call | tf_op jit(solution)/shard_map/pack/pallas_call | solution.py:47
  3.1 0.0 copy-start.1
  3.1 0.0 copy-start.3
  3.1 0.0 copy-start.4
  3.1 9.4 %all-to-all-start = ((bf16[32,3,64,128]{3,2,1,0:T(8,128)(2,1)}), bf16[32,3,64,128]{3,2,1,0:T(8,128)(2,1)S(1)}, u32[]{:S(2)}, u32[]{:S(2)}) async-start(bf16[32,3,64,128]{3,2,1,0:T(8,128)(2,1)} %bitcast.38), calls=%async_computation | async-start | bytes 3145728 | tf_op jit(solution)/shard_map/all_to_all | solution.py:325
  12.6 0.0 copy-done.1
  12.6 0.0 copy-start.2
  12.6 1.0 copy-done.2
  13.6 1.9 %conv.1 = (f32[32,512]{1,0:T(8,128)S(1)}, f32[32,512]{1,0:T(8,128)S(1)}, f32[32,512]{1,0:T(8,128)S(1)}) custom-call(bf16[512,512]{1,0:T(8,128)(2,1)S(1)} %bitcast.37, bf16[864,512]{1,0:T(8,128)(2,1)S(1)} %bitcast.36), custom_call_target="tpu_custom_call" | custom-call | flops 452984832 | bytes 2097152 | tf_op jit(solution)/shard_map/conv/pallas_call | solution.py:114
  15.5 2.2 %collective-permute-start = (f32[32,512]{1,0:T(8,128)S(1)}, f32[32,512]{1,0:T(8,128)S(1)}, u32[]{:S(2)}, u32[]{:S(2)}) collective-permute-start(f32[32,512]{1,0:T(8,128)S(1)} %get-tuple-element.23), channel_id=1, source_target_pairs={{0,1},{1,2},{2,3},{3,4},{4,5},{5,6},{6,7},{7,8},{8,9},{9,10},{10,1... | collective-permute-start | bytes 196616 | tf_op jit(solution)/shard_map/ppermute | solution.py:354
  17.7 1.3 collective-permute-start.1
  19.0 0.0 copy-done
  19.1 0.1 copy.49
  19.2 0.0 copy-done.3
  19.2 0.1 copy.45
  19.3 0.0 copy-done.4
  19.3 0.1 copy.46
  19.4 0.1 pad_bitcast_fusion.1
  19.5 0.0 copy-start.5
  19.5 32.5 %all-to-all-done.got_ref = bf16[32,3,64,128]{3,2,1,0:T(8,128)(2,1)S(1)} async-done(((bf16[32,3,64,128]{3,2,1,0:T(8,128)(2,1)}), bf16[32,3,64,128]{3,2,1,0:T(8,128)(2,1)S(1)}, u32[]{:S(2)}, u32[]{:S(2)}) %all-to-all-start) | async-done | bytes 1572896 | tf_op jit(solution)/shard_map/all_to_all | solution.py:325
  52.0 8.2 %forward.1 = (bf16[2048,2048]{1,0:T(8,128)(2,1)}, bf16[2048,128]{1,0:T(8,128)(2,1)}, f32[2048,128]{1,0:T(8,128)}, bf16[32,32,128]{2,1,0:T(8,128)(2,1)}) custom-call(bf16[32,3,64,128]{3,2,1,0:T(8,128)(2,1)S(1)} %all-to-all-done.got_ref, bf16[2,128,128]{2,1,0:T(8,128)(2,1)S(1)} %pad_maximum_fusion.w_ref), custom_call_target="tpu_custom_call" | custom-call | flops 2147483648 | bytes 12582912 | tf_op jit(solution)/shard_map/forward/pallas_call | solution.py:182
  60.2 0.0 collective-permute-done
  60.2 0.0 collective-permute-done.1
  60.2 3.9 %all-to-all-start.1 = ((bf16[16,64,128]{2,1,0:T(8,128)(2,1)}), bf16[16,64,128]{2,1,0:T(8,128)(2,1)S(1)}, u32[]{:S(2)}, u32[]{:S(2)}) async-start(bf16[16,64,128]{2,1,0:T(8,128)(2,1)} %bitcast.6), calls=%async_computation.1 | async-start | bytes 524288 | tf_op jit(solution)/shard_map/all_to_all | solution.py:325
  64.2 0.0 copy-done.5
  64.2 0.1 add_add_fusion
  64.3 0.1 copy.41
  64.4 0.3 reshape.52
  64.7 0.1 copy.51
  64.8 0.0 copy-start.6
  64.8 0.1 fusion
  64.9 0.2 copy.44
  65.1 0.2 exp.7
  65.2 0.2 copy.43
  65.4 0.2 unstack.11
  65.6 0.0 copy-done.6
  65.6 0.1 subtract_subtract_fusion
  65.7 0.1 copy.47
  65.8 0.1 copy.48
  65.8 0.1 reshape.54
  65.9 2.2 %collective-permute-start.2 = (f32[32,128]{1,0:T(8,128)S(1)}, f32[32,128]{1,0:T(8,128)S(1)}, u32[]{:S(2)}, u32[]{:S(2)}) collective-permute-start(f32[32,128]{1,0:T(8,128)S(1)} %dynamic-slice_bitcast_fusion.1), channel_id=1, source_target_pairs={{0,1},{1,0},{2,3},{3,2},{4,5},{5,4},{6,7},{7,6},{8,9},{9,8},{10,11... | collective-permute-start | bytes 49160 | tf_op jit(solution)/shard_map/ppermute | solution.py:331
  68.1 0.9 collective-permute-done.2
  69.0 8.1 %all-to-all-done.1.part_ref = bf16[16,64,128]{2,1,0:T(8,128)(2,1)S(1)} async-done(((bf16[16,64,128]{2,1,0:T(8,128)(2,1)}), bf16[16,64,128]{2,1,0:T(8,128)(2,1)S(1)}, u32[]{:S(2)}, u32[]{:S(2)}) %all-to-all-start.1) | async-done | bytes 262176 | tf_op jit(solution)/shard_map/all_to_all | solution.py:325
  77.1 14.5 %all_to_all.20 = bf16[16,64,128]{2,1,0:T(8,128)(2,1)S(1)} all-to-all(bf16[16,64,128]{2,1,0:T(8,128)(2,1)S(1)} %errors.1), channel_id=1, replica_groups={{0,2,4,6,8,10,12,14,16,18,20,22,24,26,28,30},{1,3,5,7,9,11,13,15,17,19,..., dimensions={0} | all-to-all | bytes 524288 | tf_op jit(solution)/shard_map/all_to_all | solution.py:325
  91.7 11.3 %backward.1 = (bf16[32,3,64,128]{3,2,1,0:T(8,128)(2,1)}, f32[128,128]{1,0:T(8,128)S(1)}) custom-call(bf16[32,3,64,128]{3,2,1,0:T(8,128)(2,1)S(1)} %all-to-all-done.got_ref, bf16[2,128,128]{2,1,0:T(8,128)(2,1)S(1)} %pad_maximum_fusion.w_ref, bf16[2048,2048]{1,0:T(8,128)(2,1)} %get-tuple-element.20.p_ref, bf16[2048,128]{1,0:T(8,128)(2,1)} %get-tuple-element.25.a_ref, ...), custom_call_target="tpu_custom_call" | custom-call | flops 4294967296 | bytes 14680064 | tf_op jit(solution)/shard_map/backward/pallas_call | solution.py:295
  103.0 4.0 %all-to-all-start.3 = ((bf16[32,3,64,128]{3,2,1,0:T(8,128)(2,1)}), bf16[32,3,64,128]{3,2,1,0:T(8,128)(2,1)S(1)}, u32[]{:S(2)}, u32[]{:S(2)}) async-start(bf16[32,3,64,128]{3,2,1,0:T(8,128)(2,1)} %get-tuple-element.31), calls=%async_computation.3 | async-start | bytes 3145728 | tf_op jit(solution)/shard_map/all_to_all | solution.py:325
  107.0 0.1 slice_add_fusion
  107.1 2.1 %collective-permute-start.3 = (f32[64,64]{1,0:T(8,128)S(1)}, f32[64,64]{1,0:T(8,128)S(1)}, u32[]{:S(2)}, u32[]{:S(2)}) collective-permute-start(f32[64,64]{1,0:T(8,128)S(1)} %dynamic-slice_bitcast_fusion), channel_id=1, source_target_pairs={{0,1},{1,0},{2,3},{3,2},{4,5},{5,4},{6,7},{7,6},{8,9},{9,8},{10,11... | collective-permute-start | bytes 49160 | tf_op jit(solution)/shard_map/ppermute | solution.py:331
  109.2 1.0 collective-permute-done.3
  110.2 3.0 %collective-permute-start.4 = (f32[64,64]{1,0:T(8,128)S(1)}, f32[64,64]{1,0:T(8,128)S(1)}, u32[]{:S(2)}, u32[]{:S(2)}) collective-permute-start(f32[64,64]{1,0:T(8,128)S(1)} %bitcast_add_fusion), channel_id=1, source_target_pairs={{0,32},{32,0},{64,96},{96,64},{128,160},{160,128},{192,224},{224,1... | collective-permute-start | bytes 49160 | tf_op jit(solution)/shard_map/ppermute | solution.py:331
  113.2 2.7 %collective-permute-done.4 = f32[64,64]{1,0:T(8,128)S(1)} collective-permute-done((f32[64,64]{1,0:T(8,128)S(1)}, f32[64,64]{1,0:T(8,128)S(1)}, u32[]{:S(2)}, u32[]{:S(2)}) %collective-permute-start.4) | collective-permute-done | bytes 16416 | tf_op jit(solution)/shard_map/ppermute | solution.py:331
  116.0 2.4 %collective-permute-start.5 = (f32[64,64]{1,0:T(8,128)S(1)}, f32[64,64]{1,0:T(8,128)S(1)}, u32[]{:S(2)}, u32[]{:S(2)}) collective-permute-start(f32[64,64]{1,0:T(8,128)S(1)} %add.69), channel_id=1, source_target_pairs={{0,64},{32,96},{64,0},{96,32},{128,192},{160,224},{192,128},{224,1... | collective-permute-start | bytes 49160 | tf_op jit(solution)/shard_map/ppermute | solution.py:331
  118.4 4.9 %collective-permute-done.5 = f32[64,64]{1,0:T(8,128)S(1)} collective-permute-done((f32[64,64]{1,0:T(8,128)S(1)}, f32[64,64]{1,0:T(8,128)S(1)}, u32[]{:S(2)}, u32[]{:S(2)}) %collective-permute-start.5) | collective-permute-done | bytes 16416 | tf_op jit(solution)/shard_map/ppermute | solution.py:331
  123.3 6.0 %collective-permute-start.6 = (f32[64,64]{1,0:T(8,128)S(1)}, f32[64,64]{1,0:T(8,128)S(1)}, u32[]{:S(2)}, u32[]{:S(2)}) collective-permute-start(f32[64,64]{1,0:T(8,128)S(1)} %add.70), channel_id=1, source_target_pairs={{0,128},{32,160},{64,192},{96,224},{128,0},{160,32},{192,64},{224,... | collective-permute-start | bytes 49160 | tf_op jit(solution)/shard_map/ppermute | solution.py:331
  129.4 2.0 %collective-permute-done.6 = f32[64,64]{1,0:T(8,128)S(1)} collective-permute-done((f32[64,64]{1,0:T(8,128)S(1)}, f32[64,64]{1,0:T(8,128)S(1)}, u32[]{:S(2)}, u32[]{:S(2)}) %collective-permute-start.6) | collective-permute-done | bytes 16416 | tf_op jit(solution)/shard_map/ppermute | solution.py:331
  131.4 8.9 %collective-permute-start.7 = (f32[64,64]{1,0:T(8,128)S(1)}, f32[64,64]{1,0:T(8,128)S(1)}, u32[]{:S(2)}, u32[]{:S(2)}) collective-permute-start(f32[64,64]{1,0:T(8,128)S(1)} %add.71), channel_id=1, source_target_pairs={{0,256},{32,288},{64,320},{96,352},{128,384},{160,416},{192,448},{... | collective-permute-start | bytes 49160 | tf_op jit(solution)/shard_map/ppermute | solution.py:331
  140.3 2.1 %collective-permute-done.7 = f32[64,64]{1,0:T(8,128)S(1)} collective-permute-done((f32[64,64]{1,0:T(8,128)S(1)}, f32[64,64]{1,0:T(8,128)S(1)}, u32[]{:S(2)}, u32[]{:S(2)}) %collective-permute-start.7) | collective-permute-done | bytes 16416 | tf_op jit(solution)/shard_map/ppermute | solution.py:331
  142.4 0.6 add.72
  143.1 4.3 %all-to-all-done.3 = bf16[32,3,64,128]{3,2,1,0:T(8,128)(2,1)S(1)} async-done(((bf16[32,3,64,128]{3,2,1,0:T(8,128)(2,1)}), bf16[32,3,64,128]{3,2,1,0:T(8,128)(2,1)S(1)}, u32[]{:S(2)}, u32[]{:S(2)}) %all-to-all-start.3) | async-done | bytes 1572896 | tf_op jit(solution)/shard_map/all_to_all | solution.py:325
  147.4 1.1 unpack.1
  (10 shorter events, 0.1 us)
Async XLA Ops:
  0.6 18.4 %copy-start = (bf16[2048,64]{0,1:T(8,128)(2,1)S(1)}, bf16[2048,64]{0,1:T(8,128)(2,1)}, u32[]{:S(2)}) copy-start(bf16[2048,64]{0,1:T(8,128)(2,1)} %param.18) | copy-start | bytes 786436
  3.1 9.5 %copy-start.1 = (bf16[27,512,32]{1,2,0:T(8,128)(2,1)S(1)}, bf16[27,512,32]{1,2,0:T(8,128)(2,1)}, u32[]{:S(2)}) copy-start(bf16[27,512,32]{1,2,0:T(8,128)(2,1)} %param.11) | copy-start | bytes 2654212
  3.1 16.1 %copy-start.3 = (f32[2,64,64]{2,1,0:T(8,128)S(1)}, f32[2,64,64]{2,1,0:T(8,128)}, u32[]{:S(2)}) copy-start(f32[2,64,64]{2,1,0:T(8,128)} %param.13) | copy-start | bytes 98308
  3.1 16.2 %copy-start.4 = (f32[2,64,64]{2,1,0:T(8,128)S(1)}, f32[2,64,64]{2,1,0:T(8,128)}, u32[]{:S(2)}) copy-start(f32[2,64,64]{2,1,0:T(8,128)} %param.14) | copy-start | bytes 98308
  3.1 48.9 %all-to-all-start = ((bf16[32,3,64,128]{3,2,1,0:T(8,128)(2,1)}), bf16[32,3,64,128]{3,2,1,0:T(8,128)(2,1)S(1)}, u32[]{:S(2)}, u32[]{:S(2)}) async-start(bf16[32,3,64,128]{3,2,1,0:T(8,128)(2,1)} %bitcast.38), calls=%async_computation | async-start | bytes 3145728 | tf_op jit(solution)/shard_map/all_to_all | solution.py:325
  12.6 1.0 copy-start.2
  15.5 44.7 %collective-permute-start = (f32[32,512]{1,0:T(8,128)S(1)}, f32[32,512]{1,0:T(8,128)S(1)}, u32[]{:S(2)}, u32[]{:S(2)}) collective-permute-start(f32[32,512]{1,0:T(8,128)S(1)} %get-tuple-element.23), channel_id=1, source_target_pairs={{0,1},{1,2},{2,3},{3,4},{4,5},{5,6},{6,7},{7,8},{8,9},{9,10},{10,1... | collective-permute-start | bytes 196616 | tf_op jit(solution)/shard_map/ppermute | solution.py:354
  17.7 42.5 %collective-permute-start.1 = (f32[32,512]{1,0:T(8,128)S(1)}, f32[32,512]{1,0:T(8,128)S(1)}, u32[]{:S(2)}, u32[]{:S(2)}) collective-permute-start(f32[32,512]{1,0:T(8,128)S(1)} %get-tuple-element.24), channel_id=1, source_target_pairs={{1,0},{2,1},{3,2},{4,3},{5,4},{6,5},{7,6},{8,7},{9,8},{10,9},{11,1... | collective-permute-start | bytes 196616 | tf_op jit(solution)/shard_map/ppermute | solution.py:354
  19.5 44.7 %copy-start.5 = (f32[32]{0:T(128)S(1)}, f32[32]{0:T(128)}, u32[]{:S(2)}) copy-start(f32[32]{0:T(128)} %param.12) | copy-start | bytes 388
  60.2 16.9 %all-to-all-start.1 = ((bf16[16,64,128]{2,1,0:T(8,128)(2,1)}), bf16[16,64,128]{2,1,0:T(8,128)(2,1)S(1)}, u32[]{:S(2)}, u32[]{:S(2)}) async-start(bf16[16,64,128]{2,1,0:T(8,128)(2,1)} %bitcast.6), calls=%async_computation.1 | async-start | bytes 524288 | tf_op jit(solution)/shard_map/all_to_all | solution.py:325
  64.8 0.8 copy-start.6
  65.9 3.1 %collective-permute-start.2 = (f32[32,128]{1,0:T(8,128)S(1)}, f32[32,128]{1,0:T(8,128)S(1)}, u32[]{:S(2)}, u32[]{:S(2)}) collective-permute-start(f32[32,128]{1,0:T(8,128)S(1)} %dynamic-slice_bitcast_fusion.1), channel_id=1, source_target_pairs={{0,1},{1,0},{2,3},{3,2},{4,5},{5,4},{6,7},{7,6},{8,9},{9,8},{10,11... | collective-permute-start | bytes 49160 | tf_op jit(solution)/shard_map/ppermute | solution.py:331
  103.0 44.4 %all-to-all-start.3 = ((bf16[32,3,64,128]{3,2,1,0:T(8,128)(2,1)}), bf16[32,3,64,128]{3,2,1,0:T(8,128)(2,1)S(1)}, u32[]{:S(2)}, u32[]{:S(2)}) async-start(bf16[32,3,64,128]{3,2,1,0:T(8,128)(2,1)} %get-tuple-element.31), calls=%async_computation.3 | async-start | bytes 3145728 | tf_op jit(solution)/shard_map/all_to_all | solution.py:325
  107.1 3.1 %collective-permute-start.3 = (f32[64,64]{1,0:T(8,128)S(1)}, f32[64,64]{1,0:T(8,128)S(1)}, u32[]{:S(2)}, u32[]{:S(2)}) collective-permute-start(f32[64,64]{1,0:T(8,128)S(1)} %dynamic-slice_bitcast_fusion), channel_id=1, source_target_pairs={{0,1},{1,0},{2,3},{3,2},{4,5},{5,4},{6,7},{7,6},{8,9},{9,8},{10,11... | collective-permute-start | bytes 49160 | tf_op jit(solution)/shard_map/ppermute | solution.py:331
  110.2 5.8 %collective-permute-start.4 = (f32[64,64]{1,0:T(8,128)S(1)}, f32[64,64]{1,0:T(8,128)S(1)}, u32[]{:S(2)}, u32[]{:S(2)}) collective-permute-start(f32[64,64]{1,0:T(8,128)S(1)} %bitcast_add_fusion), channel_id=1, source_target_pairs={{0,32},{32,0},{64,96},{96,64},{128,160},{160,128},{192,224},{224,1... | collective-permute-start | bytes 49160 | tf_op jit(solution)/shard_map/ppermute | solution.py:331
  116.0 7.3 %collective-permute-start.5 = (f32[64,64]{1,0:T(8,128)S(1)}, f32[64,64]{1,0:T(8,128)S(1)}, u32[]{:S(2)}, u32[]{:S(2)}) collective-permute-start(f32[64,64]{1,0:T(8,128)S(1)} %add.69), channel_id=1, source_target_pairs={{0,64},{32,96},{64,0},{96,32},{128,192},{160,224},{192,128},{224,1... | collective-permute-start | bytes 49160 | tf_op jit(solution)/shard_map/ppermute | solution.py:331
  123.3 8.1 %collective-permute-start.6 = (f32[64,64]{1,0:T(8,128)S(1)}, f32[64,64]{1,0:T(8,128)S(1)}, u32[]{:S(2)}, u32[]{:S(2)}) collective-permute-start(f32[64,64]{1,0:T(8,128)S(1)} %add.70), channel_id=1, source_target_pairs={{0,128},{32,160},{64,192},{96,224},{128,0},{160,32},{192,64},{224,... | collective-permute-start | bytes 49160 | tf_op jit(solution)/shard_map/ppermute | solution.py:331
  131.4 11.1 %collective-permute-start.7 = (f32[64,64]{1,0:T(8,128)S(1)}, f32[64,64]{1,0:T(8,128)S(1)}, u32[]{:S(2)}, u32[]{:S(2)}) collective-permute-start(f32[64,64]{1,0:T(8,128)S(1)} %add.71), channel_id=1, source_target_pairs={{0,256},{32,288},{64,320},{96,352},{128,384},{160,416},{192,448},{... | collective-permute-start | bytes 49160 | tf_op jit(solution)/shard_map/ppermute | solution.py:331
